TPU v7x, 128 devices: a whole 4x4x4 slice. The times are simulated.
128 devices in a mesh: gy: 16 (over y_hi, z, core), gz: 8 (over x, y_lo).
Axes of the slice: x: 4, y: 4 (y_hi: 2, y_lo: 2; y = y_hi * 2 + y_lo), z: 4, core: 2. Of those that a mesh axis runs over, the one named last changes fastest.
Arguments:
- field_in: bfloat16 [64, 256, 128, 256], P(None, 'gy', 'gz'), may hold values from -42 to 42
- spectral_weight: bfloat16 [32, 32, 32, 64, 128], P('gz', 'gy'), may hold values from -1.5258789e-05 to 1.5258789e-05
- point_weight: bfloat16 [64, 64], replicated, may hold values from -0.75 to 0.75
- point_bias: float32 [64], replicated, may hold values from -3 to 3
- out_weight: bfloat16 [64, 3], replicated, may hold values from -0.75 to 0.75
- out_bias: float32 [3], replicated, may hold values from -4 to 4
Outputs:
- loss_value: float32 [], replicated
- grad_spectral: float32 [32, 32, 32, 64, 128], P('gz', 'gy')
- grad_point: float32 [64, 64], replicated
- grad_point_bias: float32 [64], replicated
- grad_out: float32 [64, 3], replicated
- grad_out_bias: float32 [3], replicated
All inputs are finite; a program needn't handle non-finite values.
Results may differ from a plain program's by a relative error of at most 0.01.
Values may be sent and summed in bfloat16 or wider, within the bound.
A program may use at most 192 MiB of HBM per device.

v0:
```python
import math
import jax
import jax.numpy as jnp
from jax import lax
from jax.sharding import PartitionSpec as P

NX = 256
NY = 256
NZ = 128
MX = 32
MY = 32
MZ = 32


def with_halo(block, sides, width):
    for axis, dim in sides:
        count = lax.axis_size(axis)
        forward = [(i, i + 1) for i in range(count - 1)]
        backward = [(target, source) for source, target in forward]
        low = lax.ppermute(
            lax.slice_in_dim(block, block.shape[dim] - width, None, axis=dim), axis, forward
        )
        high = lax.ppermute(lax.slice_in_dim(block, 0, width, axis=dim), axis, backward)
        block = jnp.concatenate([low, block, high], axis=dim)
    return block


def frequencies(mode_count, mode_total):
    mode_index = jnp.arange(mode_count, dtype=jnp.int32)
    return jnp.where(mode_index < mode_total // 2, mode_index, mode_index - mode_total)


def twiddle(positions, wave_numbers, length):
    product = positions[:, None] * wave_numbers[None, :] % length
    phases = product.astype(jnp.float32) * (2.0 * math.pi / length)
    return (jnp.cos(phases).astype(jnp.bfloat16), jnp.sin(phases).astype(jnp.bfloat16))


def rotate(with_cos, with_sin, forward):
    half_width = with_cos.shape[-1] // 2
    cos_real, cos_imag = (with_cos[..., :half_width], with_cos[..., half_width:])
    sin_real, sin_imag = (with_sin[..., :half_width], with_sin[..., half_width:])
    if forward:
        return jnp.concatenate([cos_real + sin_imag, cos_imag - sin_real], axis=-1)
    return jnp.concatenate([cos_real - sin_imag, cos_imag + sin_real], axis=-1)


def x_tables(length, mode_total):
    cos_part, sin_part = twiddle(
        jnp.arange(length, dtype=jnp.int32), frequencies(mode_total, mode_total), length
    )
    forward_table = jnp.stack([cos_part, -sin_part], axis=1)
    inverse_table = jnp.stack([cos_part.T, -sin_part.T], axis=0)
    return (forward_table, inverse_table)


def cell_loss(field_b, slope_x, slope_y, slope_z):
    current_x = slope_y[2] - slope_z[1]
    current_y = slope_z[0] - slope_x[2]
    current_z = slope_x[1] - slope_y[0]
    force_x = current_y * field_b[2] - current_z * field_b[1]
    force_y = current_z * field_b[0] - current_x * field_b[2]
    force_z = current_x * field_b[1] - current_y * field_b[0]
    spread = slope_x[0] + slope_y[1] + slope_z[2]
    strength = field_b[0] * field_b[0] + field_b[1] * field_b[1] + field_b[2] * field_b[2] + 1.0
    return (force_x * force_x + force_y * force_y + force_z * force_z) / strength + spread * spread


def gelu_slope(pre_act):
    normal_cdf = 0.5 * (1.0 + lax.erf(pre_act * (1.0 / math.sqrt(2.0))))
    density = jnp.exp(-0.5 * pre_act * pre_act) * (1.0 / math.sqrt(2.0 * math.pi))
    return normal_cdf + pre_act * density


def to_modes(grid_field, factor, y_cells, z_cells, forward_table):
    channels, local_rows, local_depth = (
        grid_field.shape[0],
        grid_field.shape[1],
        grid_field.shape[2],
    )
    products = jnp.einsum(
        "cyzx,xpk->yzkpc", grid_field, forward_table, preferred_element_type=jnp.float32
    )
    x_modes = products.reshape(local_rows, local_depth, MX, 2 * channels).astype(jnp.bfloat16)
    y_cos, y_sin = twiddle(
        y_cells, frequencies(MY // lax.axis_size("gy") * lax.axis_size("gy"), MY), NY
    )
    with_cos = jnp.einsum("yzkc,yj->jzkc", x_modes, y_cos, preferred_element_type=jnp.float32)
    with_sin = jnp.einsum("yzkc,yj->jzkc", x_modes, y_sin, preferred_element_type=jnp.float32)
    y_modes = lax.psum_scatter(
        rotate(with_cos, with_sin, True), "gy", scatter_dimension=0, tiled=True
    ).astype(jnp.bfloat16)
    z_cos, z_sin = twiddle(
        z_cells, frequencies(MZ // lax.axis_size("gz") * lax.axis_size("gz"), MZ), NZ
    )
    with_cos = jnp.einsum("bzkc,zj->jbkc", y_modes, z_cos, preferred_element_type=jnp.float32)
    with_sin = jnp.einsum("bzkc,zj->jbkc", y_modes, z_sin, preferred_element_type=jnp.float32)
    summed = lax.psum_scatter(
        rotate(with_cos, with_sin, True), "gz", scatter_dimension=0, tiled=True
    )
    return (summed * factor).astype(jnp.bfloat16)


def from_modes(modes_out, y_cells, z_cells):
    portion = lax.all_gather(modes_out, "gz", axis=0, tiled=True)
    z_cos, z_sin = twiddle(z_cells, frequencies(portion.shape[0], MZ), NZ)
    with_cos = jnp.einsum("jbkc,zj->bzkc", portion, z_cos, preferred_element_type=jnp.float32)
    with_sin = jnp.einsum("jbkc,zj->bzkc", portion, z_sin, preferred_element_type=jnp.float32)
    z_back = rotate(with_cos, with_sin, False).astype(jnp.bfloat16)
    portion = lax.all_gather(z_back, "gy", axis=0, tiled=True)
    y_cos, y_sin = twiddle(y_cells, frequencies(portion.shape[0], MY), NY)
    with_cos = jnp.einsum("jzkc,yj->yzkc", portion, y_cos, preferred_element_type=jnp.float32)
    with_sin = jnp.einsum("jzkc,yj->yzkc", portion, y_sin, preferred_element_type=jnp.float32)
    return rotate(with_cos, with_sin, False).astype(jnp.bfloat16)


def mix_modes(modes_in, spectral_weight):
    channels = spectral_weight.shape[-2]
    with_real = jnp.einsum(
        "abki,abkio->abko",
        modes_in[..., :channels],
        spectral_weight,
        preferred_element_type=jnp.float32,
    )
    with_imag = jnp.einsum(
        "abki,abkio->abko",
        modes_in[..., channels:],
        spectral_weight,
        preferred_element_type=jnp.float32,
    )
    return jnp.concatenate(
        [
            with_real[..., :channels] - with_imag[..., channels:],
            with_real[..., channels:] + with_imag[..., :channels],
        ],
        axis=-1,
    ).astype(jnp.bfloat16)


def weight_grad(modes_in, grad_modes):
    channels = modes_in.shape[-1] // 2
    with_real = jnp.einsum(
        "abki,abko->abkio", modes_in[..., :channels], grad_modes, preferred_element_type=jnp.float32
    )
    with_imag = jnp.einsum(
        "abki,abko->abkio", modes_in[..., channels:], grad_modes, preferred_element_type=jnp.float32
    )
    return jnp.concatenate(
        [
            with_real[..., :channels] + with_imag[..., channels:],
            with_real[..., channels:] - with_imag[..., :channels],
        ],
        axis=-1,
    )


def on_device(field_in, spectral_weight, point_weight, point_bias, out_weight, out_bias):
    channels, local_rows, local_depth, x_count = field_in.shape
    y_cells = lax.axis_index("gy") * local_rows + jnp.arange(local_rows, dtype=jnp.int32)
    z_cells = lax.axis_index("gz") * local_depth + jnp.arange(local_depth, dtype=jnp.int32)
    forward_table, inverse_table = x_tables(x_count, MX)
    modes_in = to_modes(
        field_in, math.sqrt(MX * MY * MZ / (NX * NY * NZ)), y_cells, z_cells, forward_table
    )
    modes_out = mix_modes(modes_in, spectral_weight)
    y_back = from_modes(modes_out, y_cells, z_cells)
    spectral = jnp.einsum(
        "yzkpc,pkx->cyzx",
        y_back.reshape(local_rows, local_depth, MX, 2, channels),
        inverse_table,
        preferred_element_type=jnp.float32,
    )
    pointwise = jnp.einsum(
        "cyzx,co->oyzx", field_in, point_weight, preferred_element_type=jnp.float32
    )
    pre_act = spectral + pointwise + point_bias[:, None, None, None]
    hidden = jax.nn.gelu(pre_act, approximate=False).astype(jnp.bfloat16)
    b_field = (
        jnp.einsum("cyzx,cb->byzx", hidden, out_weight, preferred_element_type=jnp.float32)
        + out_bias[:, None, None, None]
    )
    padded = with_halo(b_field, (("gy", 1), ("gz", 2)), 2)
    widened = padded[:, 1:-1, 1:-1]
    x_padded = jnp.pad(widened, ((0, 0), (0, 0), (0, 0), (1, 1)))
    slope_x = (x_padded[..., 2:] - x_padded[..., :-2]) * 0.5
    slope_y = (padded[:, 2:, 1:-1] - padded[:, :-2, 1:-1]) * 0.5
    slope_z = (padded[:, 1:-1, 2:] - padded[:, 1:-1, :-2]) * 0.5
    cell_terms, pullback = jax.vjp(cell_loss, widened, slope_x, slope_y, slope_z)
    y_wide = lax.axis_index("gy") * local_rows - 1 + jnp.arange(local_rows + 2, dtype=jnp.int32)
    z_wide = lax.axis_index("gz") * local_depth - 1 + jnp.arange(local_depth + 2, dtype=jnp.int32)
    inside = ((y_wide >= 0) & (y_wide < NY))[:, None] & ((z_wide >= 0) & (z_wide < NZ))[None, :]
    weight_map = jnp.broadcast_to(
        jnp.where(inside, 1.0, 0.0)[:, :, None] / (NX * NY * NZ), cell_terms.shape
    ).astype(jnp.float32)
    grad_wide, grad_x, grad_y, grad_z = pullback(weight_map)
    gx_inner = jnp.pad(grad_x[:, 1:-1, 1:-1], ((0, 0), (0, 0), (0, 0), (1, 1)))
    grad_b = grad_wide[:, 1:-1, 1:-1] + (gx_inner[..., :-2] - gx_inner[..., 2:]) * 0.5
    grad_b = grad_b + (grad_y[:, :-2, 1:-1] - grad_y[:, 2:, 1:-1]) * 0.5
    grad_b = grad_b + (grad_z[:, 1:-1, :-2] - grad_z[:, 1:-1, 2:]) * 0.5
    loss_local = jnp.sum(cell_terms[1:-1, 1:-1])
    weights_f = out_weight.astype(jnp.float32)
    grad_hidden = jnp.zeros_like(pre_act)
    for component in range(3):
        grad_hidden = (
            grad_hidden + weights_f[:, component][:, None, None, None] * grad_b[component][None]
        )
    grad_pre = (grad_hidden * gelu_slope(pre_act)).astype(jnp.bfloat16)
    out_part = jnp.einsum(
        "cyzx,byzx->cb",
        hidden,
        grad_b,
        preferred_element_type=jnp.float32,
        precision=lax.Precision.HIGHEST,
    )
    out_bias_part = jnp.sum(grad_b, axis=(1, 2, 3))
    point_part = jnp.einsum("iyzx,oyzx->io", field_in, grad_pre, preferred_element_type=jnp.float32)
    point_bias_part = jnp.sum(grad_pre.astype(jnp.float32), axis=(1, 2, 3))
    totals = lax.psum(
        (loss_local, point_part, point_bias_part, out_part, out_bias_part), ("gy", "gz")
    )
    grad_modes = to_modes(grad_pre, 1.0, y_cells, z_cells, forward_table)
    grad_spectral = weight_grad(modes_in, grad_modes)
    return (totals[0] / (NX * NY * NZ), grad_spectral, totals[1], totals[2], totals[3], totals[4])


def solution(mesh):
    return jax.shard_map(
        on_device,
        mesh=mesh,
        in_specs=(P(None, "gy", "gz", None), P("gz", "gy", None, None, None), P(), P(), P(), P()),
        out_specs=(P(), P("gz", "gy", None, None, None), P(), P(), P(), P()),
        check_vma=False,
    )
```

profile of v0, /device:TPU:1, one launch (start us, length us, event | category | flops | bytes accessed | tf_op | source)
XLA Modules:
  0.0 781.1 jit_solution(12357975820388527888)
XLA Ops:
  7.7 13.6 %convert_bitcast_fusion.1 = bf16[16,16,32,2,64]{4,2,1,0,3:T(8,128)(2,1)S(1)} fusion(bf16[64,16,16,256]{3,2,1,0:T(8,128)(2,1)} %param.6, bf16[256,1,32]{0,2,1:T(8,128)(2,1)S(1)} %fusion.88, bf16[256,1,32]{0,2,1:T(8,128)(2,1)S(1)} %cosine_convert_fusion), kind=kOutput, calls=%fused_computation.58 | convolution fusion | flops 537985024 | bytes 10518528 | tf_op jit(solution)/shard_map/cyzx,xpk->yzkpc/dot_general | solution.py:81
  21.2 6.8 copy.89
  28.0 6.8 reshape.338
  34.8 4.8 fusion.109
  39.6 4.7 fusion.114
  44.3 18.8 %slice_add_fusion.2 = (f32[32,16,32,64]{3,0,2,1:T(8,128)}, f32[32,16,32,64]{3,0,2,1:T(8,128)}) fusion(f32[32,16,32,128]{3,0,2,1:T(8,128)} %fusion.109, f32[32,16,32,128]{3,0,2,1:T(8,128)} %fusion.114), kind=kLoop, calls=%fused_computation.36 | loop fusion | flops 2097152 | bytes 25165824 | tf_op jit(solution)/shard_map/add | solution.py:44
  63.1 11.4 %pad_maximum_fusion = f32[32,16,32,128]{3,0,2,1:T(8,128)} fusion(f32[32,16,32,64]{3,0,2,1:T(8,128)} %get-tuple-element.63, f32[32,16,32,64]{3,0,2,1:T(8,128)} %get-tuple-element.62), kind=kLoop, calls=%fused_computation.37 | loop fusion | flops 2097152 | bytes 16777216 | tf_op jit(solution)/shard_map/concatenate | solution.py:44
  74.5 11.5 %copy.52 = f32[32,16,32,128]{3,2,1,0:T(8,128)} copy(f32[32,16,32,128]{3,0,2,1:T(8,128)} %pad_maximum_fusion) | data formatting | bytes 16777216 | tf_op jit(solution)/shard_map/concatenate | solution.py:44
  86.1 104.2 %reduce-scatter.5.cloned.1.call-done = f32[2,16,32,128]{3,2,1,0:T(8,128)} async-done(((f32[32,16,32,128]{3,2,1,0:T(8,128)}), f32[2,16,32,128]{3,2,1,0:T(8,128)}) %reduce-scatter.5.cloned.1.call-update) | async-done | bytes 524304 | tf_op jit(solution)/shard_map/reduce_scatter | solution.py:90
  190.3 1.1 convert_element_type.167
  193.3 1.6 copy.55
  194.9 34.7 %reduce-scatter.7.cloned.1.call-done = f32[4,2,32,128]{3,2,1,0:T(8,128)} async-done(((f32[32,2,32,128]{3,2,1,0:T(8,128)}), f32[4,2,32,128]{3,2,1,0:T(8,128)}) %reduce-scatter.7.cloned.1.call-update) | async-done | bytes 131088 | tf_op jit(solution)/shard_map/reduce_scatter | solution.py:98
  229.6 0.9 multiply_convert_fusion
  230.6 0.7 slice_convert_fusion.1
  231.3 3.4 fusion.69
  234.7 3.4 fusion.71
  238.3 23.3 %all_gather.6 = bf16[32,2,32,128]{3,2,1,0:T(8,128)(2,1)S(1)} all-gather(bf16[4,2,32,128]{3,2,1,0:T(8,128)(2,1)S(1)} %pad_maximum_fusion.17), channel_id=1, replica_groups=mesh['gy'=16,'gz'=8] {'gz'}, dimensions={0}, use_global_device_ids=true | all-gather | bytes 589824 | tf_op jit(solution)/shard_map/all_gather | solution.py:105
  263.0 0.8 copy.58
  264.3 65.5 %all-gather.2.cloned.1.call-done = bf16[32,16,32,128]{3,2,1,0:T(8,128)(2,1)} async-done(((bf16[2,16,32,128]{3,2,1,0:T(8,128)(2,1)}), bf16[32,16,32,128]{3,2,1,0:T(8,128)(2,1)}) %all-gather.2.cloned.1.call-update) | async-done | bytes 4194320 | tf_op jit(solution)/shard_map/all_gather | solution.py:110
  329.8 4.9 fusion.29
  334.7 2.5 fusion.31
  337.2 2.6 fusion.37
  339.8 0.9 pad_maximum_fusion.3
  340.8 8.1 %fusion.27 = f32[256,16,16,64,1]{0,3,4,2,1:T(8,128)} fusion(bf16[16,16,32,2,64]{4,0,2,1,3:T(8,128)(2,1)S(1)} %pad_maximum_fusion.3, bf16[1,32,256]{2,1,0:T(8,128)(2,1)S(1)} %fusion.87, bf16[1,32,256]{2,1,0:T(8,128)(2,1)S(1)} %cosine_convert_fusion.1), kind=kOutput, calls=%fused_computation.53 | convolution fusion | flops 536936448 | bytes 18907136 | tf_op jit(solution)/shard_map/yzkpc,pkx->cyzx/dot_general | solution.py:167
  348.9 19.3 %fusion.16 = (u16[64,16,256]{2,0,1:T(8,128)(2,1)S(1)}, f32[64,16,16,256]{3,0,2,1:T(8,128)}) fusion(f32[64]{0:T(128)S(1)} %copy-done.9, bf16[64,16,16,256]{3,2,1,0:T(8,128)(2,1)} %param.6, bf16[64,64]{1,0:T(8,128)(2,1)S(1)} %copy-done, f32[256,16,16,64,1]{0,3,4,2,1:T(8,128)} %fusion.27), kind=kOutput, calls=%fused_computation.30 | convolution fusion | flops 574357504 | bytes 42475776 | tf_op jit(solution)/shard_map/cyzx,co->oyzx/dot_general | solution.py:173
  368.2 39.0 %fusion.2 = bf16[64,16,16,256]{3,0,2,1:T(8,128)(2,1)S(1)} fusion(f32[64,16,16,256]{3,0,2,1:T(8,128)} %get-tuple-element.123, u16[64,16,256]{2,0,1:T(8,128)(2,1)S(1)} %get-tuple-element.122), kind=kLoop, calls=%fused_computation.4 | loop fusion | flops 285212672 | bytes 25690112 | tf_op jit(solution)/shard_map/convert_element_type | solution.py:177
  407.3 1.2 fusion.39
  408.6 2.0 collective-permute-start
  410.5 2.4 collective-permute-start.1
  413.0 3.8 collective-permute-done.1
  416.9 2.2 collective-permute-start.3
  419.1 1.3 collective-permute-start.2
  420.5 0.9 collective-permute-done.3
  421.4 4.4 collective-permute-done.2
  426.7 1.4 fusion.41
  428.1 0.8 fusion.44
  428.9 4.9 add_multiply_fusion
  433.8 1.3 negate_multiply_fusion.3
  435.1 1.1 negate_multiply_fusion.1
  436.2 2.8 slice_multiply_fusion.1
  439.1 1.0 add_add_fusion
  440.7 1.5 pad_add_fusion.1
  442.2 3.9 fusion.168
  446.2 0.8 fusion.175
  447.1 11.2 %convert_reduce_fusion = (f32[64]{0:T(128)S(1)}, bf16[64,16,16,256]{3,0,2,1:T(8,128)(2,1)S(1)}) fusion(f32[64,16,16,256]{3,0,2,1:T(8,128)S(1)} %bitcast.132, f32[16,16,256]{2,1,0:T(8,128)S(1)} %bitcast.135, f32[64]{0:T(128)S(1)} %get-tuple-element.120, f32[16,16,256]{2,1,0:T(8,128)S(1)} %bitcast.136, f32[64]{0:T(128)S(1)} %get-tuple-element.121, ...), kind=kLoop, calls=%fused_computation.15 | loop fusion | flops 71303104 | bytes 25953280 | tf_op jit(solution)/shard_map/reduce_sum | solution.py:217
  458.3 3.4 copy-done.3
  461.7 4.1 convert_bitcast_fusion
  465.8 6.3 copy.91
  472.1 7.2 reshape.339
  479.3 4.6 fusion.106
  483.9 4.6 fusion.111
  488.6 18.5 %slice_add_fusion.1 = (f32[32,16,32,64]{3,0,2,1:T(8,128)}, f32[32,16,32,64]{3,0,2,1:T(8,128)}) fusion(f32[32,16,32,128]{3,0,2,1:T(8,128)} %fusion.106, f32[32,16,32,128]{3,0,2,1:T(8,128)} %fusion.111), kind=kLoop, calls=%fused_computation.34 | loop fusion | flops 2097152 | bytes 25165824 | tf_op jit(solution)/shard_map/add | solution.py:44
  507.1 11.2 %pad_maximum_fusion.1 = f32[32,16,32,128]{3,0,2,1:T(8,128)} fusion(f32[32,16,32,64]{3,0,2,1:T(8,128)} %get-tuple-element.61, f32[32,16,32,64]{3,0,2,1:T(8,128)} %get-tuple-element.60), kind=kLoop, calls=%fused_computation.38 | loop fusion | flops 2097152 | bytes 16777216 | tf_op jit(solution)/shard_map/concatenate | solution.py:44
  518.3 11.5 %copy.67 = f32[32,16,32,128]{3,2,1,0:T(8,128)} copy(f32[32,16,32,128]{3,0,2,1:T(8,128)} %pad_maximum_fusion.1) | data formatting | bytes 16777216 | tf_op jit(solution)/shard_map/concatenate | solution.py:44
  529.9 104.6 %reduce-scatter.9.cloned.1.call-done = f32[2,16,32,128]{3,2,1,0:T(8,128)} async-done(((f32[32,16,32,128]{3,2,1,0:T(8,128)}), f32[2,16,32,128]{3,2,1,0:T(8,128)}) %reduce-scatter.9.cloned.1.call-update) | async-done | bytes 524304 | tf_op jit(solution)/shard_map/reduce_scatter | solution.py:90
  634.6 1.1 convert_element_type.176
  637.5 1.6 copy.70
  639.8 9.0 %convolution_bitcast_fusion.2 = f32[64,3]{0,1:T(4,128)S(1)} fusion(bf16[64,16,16,256]{3,0,2,1:T(8,128)(2,1)} %copy-done.2, f32[3,16,16,256]{3,0,2,1:T(4,128)S(1)} %get-tuple-element.30), kind=kOutput, calls=%fused_computation.91 | convolution fusion | flops 150994944 | bytes 9175808 | tf_op jit(solution)/shard_map/cyzx,byzx->cb/dot_general | solution.py:208
  648.9 15.3 %fusion.45 = f32[64,64]{0,1:T(8,128)S(1)} fusion(bf16[64,16,16,256]{3,0,2,1:T(8,128)(2,1)} %copy-done.3, bf16[64,16,16,256]{3,2,1,0:T(8,128)(2,1)} %param.6), kind=kOutput, calls=%fused_computation.90 | convolution fusion | flops 536870912 | bytes 16793600 | tf_op jit(solution)/shard_map/iyzx,oyzx->io/dot_general | solution.py:216
  664.2 66.3 %all-reduce.20 = (f32[]{:T(128)}, f32[64,64]{0,1:T(8,128)S(1)}, f32[64]{0:T(128)}, f32[64,3]{0,1:T(4,128)}, f32[3]{0:T(128)}) all-reduce(f32[]{:T(128)} %slice_reduce_fusion, f32[64,64]{0,1:T(8,128)S(1)} %fusion.45, f32[64]{0:T(128)S(1)} %get-tuple-element.31, ...), channel_id=1, replica_groups=mesh['gy'=16,'gz'=8] {'gy','gz'}, use_global_device_ids=true, to_apply=%region_3.4 | all-reduce | flops 4356 | bytes 34848 | tf_op jit(solution)/shard_map/psum | solution.py:218
  731.9 0.9 convert_convert_fusion
  732.8 8.4 %broadcast_multiply_fusion.1 = (f32[4,2,32,64,128]{4,3,2,1,0:T(8,128)}, f32[4,2,32,64,128]{4,3,2,1,0:T(8,128)}) fusion(f32[4,2,32,128]{3,2,1,0:T(8,128)S(1)} %convert_convert_fusion, f32[4,2,32,64]{3,2,1,0:T(8,128)S(1)} %copy-done.5, f32[4,2,32,64]{3,2,1,0:T(8,128)S(1)} %copy-done.6), kind=kLoop, calls=%fused_computation.56 | loop fusion | flops 4194304 | bytes 17039360 | tf_op jit(solution)/shard_map/abki,abko->abkio/dot_general | solution.py:142
  741.2 19.9 %slice_add_fusion = (f32[4,2,32,64,64]{4,3,2,1,0:T(8,128)}, f32[4,2,32,64,64]{4,3,2,1,0:T(8,128)}) fusion(f32[4,2,32,64,128]{4,3,2,1,0:T(8,128)} %get-tuple-element.114, f32[4,2,32,64,128]{4,3,2,1,0:T(8,128)} %get-tuple-element.113), kind=kLoop, calls=%fused_computation.32 | loop fusion | flops 2097152 | bytes 25165824 | tf_op jit(solution)/shard_map/add | solution.py:150
  761.1 12.1 %pad_maximum_fusion.2 = f32[4,2,32,64,128]{4,3,2,1,0:T(8,128)} fusion(f32[4,2,32,64,64]{4,3,2,1,0:T(8,128)} %get-tuple-element.59, f32[4,2,32,64,64]{4,3,2,1,0:T(8,128)} %get-tuple-element.58), kind=kLoop, calls=%fused_computation.39 | loop fusion | flops 2097152 | bytes 16777216 | tf_op jit(solution)/shard_map/concatenate | solution.py:148
  (76 shorter events, 9.8 us)
Async XLA Ops:
  7.2 341.8 %copy-start = (bf16[64,64]{1,0:T(8,128)(2,1)S(1)}, bf16[64,64]{1,0:T(8,128)(2,1)}, u32[]{:S(2)}) copy-start(bf16[64,64]{1,0:T(8,128)(2,1)} %param.8) | copy-start | bytes 24580
  7.2 183.1 %reduce-scatter.5.cloned.1.call-start = ((), (), s32[]{:S(2)}) async-start(), calls=%async_computation.4 | async-start | bytes 8912896 | tf_op jit(solution)/shard_map/reduce_scatter | solution.py:90
  86.0 143.6 %reduce-scatter.7.cloned.1.call-start = ((), (), s32[]{:S(2)}) async-start(), calls=%async_computation.5 | async-start | bytes 1179648 | tf_op jit(solution)/shard_map/reduce_scatter | solution.py:98
  194.9 135.0 %all-gather.2.cloned.1.call-start = ((), (), s32[]{:S(2)}) async-start(), calls=%async_computation.6 | async-start | bytes 4456448 | tf_op jit(solution)/shard_map/all_gather | solution.py:110
  263.8 370.7 %reduce-scatter.9.cloned.1.call-start = ((), (), s32[]{:S(2)}) async-start(), calls=%async_computation.7 | async-start | bytes 8912896 | tf_op jit(solution)/shard_map/reduce_scatter | solution.py:90
  329.8 4.9 copy-start.4
  340.8 8.1 %copy-start.9 = (f32[64]{0:T(128)S(1)}, f32[64]{0:T(128)}, u32[]{:S(2)}) copy-start(f32[64]{0:T(128)} %param.9) | copy-start | bytes 772
  368.2 39.1 %copy-start.7 = (bf16[64,3]{0,1:T(4,128)(2,1)S(1)}, bf16[64,3]{0,1:T(4,128)(2,1)}, u32[]{:S(2)}) copy-start(bf16[64,3]{0,1:T(4,128)(2,1)} %param.10) | copy-start | bytes 1156
  368.2 39.1 %copy-start.8 = (f32[3]{0:T(128)S(1)}, f32[3]{0:T(128)}, u32[]{:S(2)}) copy-start(f32[3]{0:T(128)} %param.11) | copy-start | bytes 40
  407.3 9.6 %copy-start.2 = (bf16[64,16,16,256]{3,0,2,1:T(8,128)(2,1)}, bf16[64,16,16,256]{3,0,2,1:T(8,128)(2,1)S(1)}, u32[]{:S(2)}) copy-start(bf16[64,16,16,256]{3,0,2,1:T(8,128)(2,1)S(1)} %fusion.2) | copy-start | bytes 25165828
  408.6 4.4 collective-permute-start
  410.5 6.3 collective-permute-start.1
  416.9 4.5 collective-permute-start.3
  419.1 6.7 collective-permute-start.2
  435.1 12.0 %slice-start = ((s8[16777216]{0:T(1024)(128)(4,1)}), s8[4194304]{0:T(1024)(128)(4,1)S(1)}, s32[]{:S(2)}) async-start(s8[16777216]{0:T(1024)(128)(4,1)} %bitcast.131), calls=%async_computation.9 | async-start | bytes 8388608
  436.2 10.8 %slice-start.1 = ((s8[16777216]{0:T(1024)(128)(4,1)}), s8[4194304]{0:T(1024)(128)(4,1)S(1)}, s32[]{:S(2)}) async-start(s8[16777216]{0:T(1024)(128)(4,1)} %bitcast.131), calls=%async_computation.10 | async-start | bytes 8388608
  440.7 6.4 slice-start.2
  442.2 4.8 slice-start.3
  458.3 3.4 copy-start.3
  529.9 202.0 %reduce-scatter.11.cloned.1.call-start = ((), (), s32[]{:S(2)}) async-start(), calls=%async_computation.8 | async-start | bytes 1179648 | tf_op jit(solution)/shard_map/reduce_scatter | solution.py:98
  648.8 83.9 %copy-start.5 = (f32[4,2,32,64]{3,2,1,0:T(8,128)S(1)}, f32[4,2,32,64]{3,2,1,0:T(8,128)}, u32[]{:S(2)}) copy-start(f32[4,2,32,64]{3,2,1,0:T(8,128)} %get-tuple-element.115) | copy-start | bytes 196612
  648.9 83.9 %copy-start.6 = (f32[4,2,32,64]{3,2,1,0:T(8,128)S(1)}, f32[4,2,32,64]{3,2,1,0:T(8,128)}, u32[]{:S(2)}) copy-start(f32[4,2,32,64]{3,2,1,0:T(8,128)} %get-tuple-element.116) | copy-start | bytes 196612
  761.1 12.1 %copy-start.1 = (bf16[64,64]{1,0:T(8,128)(2,1)S(1)}, bf16[64,64]{1,0:T(8,128)(2,1)}, u32[]{:S(2)}) copy-start(bf16[64,64]{1,0:T(8,128)(2,1)} %param.8) | copy-start | bytes 24580
Sparse Core Ops, SparseCore 0:
  86.1 104.1 reduce-scatter.4
  195.0 34.5 reduce-scatter.6
  263.9 65.8 all-gather.1
  530.0 104.5 reduce-scatter.8
  639.2 34.5 reduce-scatter.10
where the time goes:
time: 790 us; the launch traced here: 781 us
  waiting for transfers between devices  318 us (40%)
  other arithmetic  183 us (23%)
  matrix products  106 us (13%)
  blocking collectives  89.6 us (11%)
  local copies, waits for them, and re-layouts  59.1 us (7%)
  between operations  16.3 us (2%)
  starting transfers between devices  8.05 us (1%)
    reduce_scatter x2, waiting for transfers between devices, to_modes(): lax.psum_scatter(rotate(with_cos, with_sin, True), 'gy', scatter_dimensio...  209 us
    psum x1, blocking collectives, on_device(): lax.psum((loss_local, point_part, point_bias_part, out_part, out_bias_par...  66.3 us
    all_gather x1, waiting for transfers between devices, from_modes(): portion = lax.all_gather(z_back, 'gy', axis=0, tiled=True)  65.5 us
    convert_element_type x1, other arithmetic, on_device(): hidden = jax.nn.gelu(pre_act, approximate=False).astype(jnp.bfloat16)  39 us
    add x4, other arithmetic, rotate(): return jnp.concatenate([cos_real + sin_imag, cos_imag - sin_real], axis=-1)  38.6 us
    reduce_scatter x2, waiting for transfers between devices, to_modes(): lax.psum_scatter(rotate(with_cos, with_sin, True), 'gz', scatter_dimensio...  34.7 us
    convert_element_type x4, local copies, waits for them, and re-layouts, to_modes(): products.reshape(local_rows, local_depth, MX, 2 * channels)  27 us
    concatenate x4, local copies, waits for them, and re-layouts, rotate(): return jnp.concatenate([cos_real + sin_imag, cos_imag - sin_real], axis=-1)  26.2 us
  transfers between devices with their start and end apart: 9, of which 7 were waited for; matrix products, arithmetic and copies ran while one was open for 3% of the time, Pallas kernels for 0%

commit v1 on v0

--- a/solution.py
+++ b/solution.py
@@ -216,7 +216,7 @@
     point_part = jnp.einsum("iyzx,oyzx->io", field_in, grad_pre, preferred_element_type=jnp.float32)
     point_bias_part = jnp.sum(grad_pre.astype(jnp.float32), axis=(1, 2, 3))
     totals = lax.psum(
-        (loss_local, point_part, point_bias_part, out_part, out_bias_part), ("gy", "gz")
+        lax.psum((loss_local, point_part, point_bias_part, out_part, out_bias_part), "gy"), "gz"
     )
     grad_modes = to_modes(grad_pre, 1.0, y_cells, z_cells, forward_table)
     grad_spectral = weight_grad(modes_in, grad_modes)

time: 790 us -> 827 us (1.047)
  the two profiles are of different devices: /device:TPU:1 before, /device:TPU:0 now
where the time goes in v1:
time: 827 us; the launch traced here: 818 us
  waiting for transfers between devices  314 us (38%)
  other arithmetic  183 us (22%)
  blocking collectives  132 us (16%)
  matrix products  106 us (13%)
  local copies, waits for them, and re-layouts  58.8 us (7%)
  between operations  16.3 us (2%)
    reduce_scatter x2, waiting for transfers between devices, to_modes(): lax.psum_scatter(rotate(with_cos, with_sin, True), 'gy', scatter_dimensio...  213 us
    psum x1, blocking collectives, on_device(): lax.psum((loss_local, point_part, point_bias_part, out_part, out_bias_par...  66.2 us
    all_gather x1, waiting for transfers between devices, from_modes(): portion = lax.all_gather(z_back, 'gy', axis=0, tiled=True)  53.8 us
    convert_element_type x1, other arithmetic, on_device(): hidden = jax.nn.gelu(pre_act, approximate=False).astype(jnp.bfloat16)  38.8 us
    reduce_scatter x2, waiting for transfers between devices, to_modes(): lax.psum_scatter(rotate(with_cos, with_sin, True), 'gz', scatter_dimensio...  38.8 us
    add x4, other arithmetic, rotate(): return jnp.concatenate([cos_real + sin_imag, cos_imag - sin_real], axis=-1)  38.7 us
    psum x1, blocking collectives, on_device(): lax.psum(lax.psum((loss_local, point_part, point_bias_part, out_part, out...  36.1 us
    all_gather x1, blocking collectives, from_modes(): portion = lax.all_gather(modes_out, 'gz', axis=0, tiled=True)  29.3 us
  transfers between devices with their start and end apart: 9, of which 7 were waited for; matrix products, arithmetic and copies ran while one was open for 3% of the time, Pallas kernels for 0%

profile of v1, /device:TPU:0, one launch (start us, length us, event | category | flops | bytes accessed | tf_op | source)
XLA Modules:
  0.0 817.7 jit_solution(8700051561253048024)
XLA Ops:
  7.7 13.6 %convert_bitcast_fusion.1 = bf16[16,16,32,2,64]{4,2,1,0,3:T(8,128)(2,1)S(1)} fusion(bf16[64,16,16,256]{3,2,1,0:T(8,128)(2,1)} %param.6, bf16[256,1,32]{0,2,1:T(8,128)(2,1)S(1)} %fusion.88, bf16[256,1,32]{0,2,1:T(8,128)(2,1)S(1)} %cosine_convert_fusion), kind=kOutput, calls=%fused_computation.58 | convolution fusion | flops 537985024 | bytes 10518528 | tf_op jit(solution)/shard_map/cyzx,xpk->yzkpc/dot_general | solution.py:81
  21.2 6.5 copy.89
  27.7 6.8 reshape.338
  34.5 4.8 fusion.109
  39.3 4.7 fusion.114
  44.0 18.8 %slice_add_fusion.2 = (f32[32,16,32,64]{3,0,2,1:T(8,128)}, f32[32,16,32,64]{3,0,2,1:T(8,128)}) fusion(f32[32,16,32,128]{3,0,2,1:T(8,128)} %fusion.109, f32[32,16,32,128]{3,0,2,1:T(8,128)} %fusion.114), kind=kLoop, calls=%fused_computation.36 | loop fusion | flops 2097152 | bytes 25165824 | tf_op jit(solution)/shard_map/add | solution.py:44
  62.8 11.4 %pad_maximum_fusion = f32[32,16,32,128]{3,0,2,1:T(8,128)} fusion(f32[32,16,32,64]{3,0,2,1:T(8,128)} %get-tuple-element.68, f32[32,16,32,64]{3,0,2,1:T(8,128)} %get-tuple-element.67), kind=kLoop, calls=%fused_computation.37 | loop fusion | flops 2097152 | bytes 16777216 | tf_op jit(solution)/shard_map/concatenate | solution.py:44
  74.2 11.5 %copy.52 = f32[32,16,32,128]{3,2,1,0:T(8,128)} copy(f32[32,16,32,128]{3,0,2,1:T(8,128)} %pad_maximum_fusion) | data formatting | bytes 16777216 | tf_op jit(solution)/shard_map/concatenate | solution.py:44
  85.8 105.0 %reduce-scatter.5.cloned.1.call-done = f32[2,16,32,128]{3,2,1,0:T(8,128)} async-done(((f32[32,16,32,128]{3,2,1,0:T(8,128)}), f32[2,16,32,128]{3,2,1,0:T(8,128)}) %reduce-scatter.5.cloned.1.call-update) | async-done | bytes 524304 | tf_op jit(solution)/shard_map/reduce_scatter | solution.py:90
  190.8 1.1 convert_element_type.167
  193.7 1.6 copy.55
  195.4 38.7 %reduce-scatter.7.cloned.1.call-done = f32[4,2,32,128]{3,2,1,0:T(8,128)} async-done(((f32[32,2,32,128]{3,2,1,0:T(8,128)}), f32[4,2,32,128]{3,2,1,0:T(8,128)}) %reduce-scatter.7.cloned.1.call-update) | async-done | bytes 131088 | tf_op jit(solution)/shard_map/reduce_scatter | solution.py:98
  234.1 0.9 multiply_convert_fusion
  235.8 3.4 fusion.69
  239.2 3.4 fusion.71
  242.8 29.3 %all_gather.6 = bf16[32,2,32,128]{3,2,1,0:T(8,128)(2,1)S(1)} all-gather(bf16[4,2,32,128]{3,2,1,0:T(8,128)(2,1)S(1)} %pad_maximum_fusion.17), channel_id=1, replica_groups=mesh['gy'=16,'gz'=8] {'gz'}, dimensions={0}, use_global_device_ids=true | all-gather | bytes 589824 | tf_op jit(solution)/shard_map/all_gather | solution.py:105
  273.6 0.8 copy.58
  274.9 53.8 %all-gather.2.cloned.1.call-done = bf16[32,16,32,128]{3,2,1,0:T(8,128)(2,1)} async-done(((bf16[2,16,32,128]{3,2,1,0:T(8,128)(2,1)}), bf16[32,16,32,128]{3,2,1,0:T(8,128)(2,1)}) %all-gather.2.cloned.1.call-update) | async-done | bytes 4194320 | tf_op jit(solution)/shard_map/all_gather | solution.py:110
  328.6 4.9 fusion.29
  333.5 2.5 fusion.31
  336.0 2.5 fusion.37
  338.6 0.9 pad_maximum_fusion.3
  339.5 8.1 fusion.27
  347.7 19.3 %fusion.16 = (u16[64,16,256]{2,0,1:T(8,128)(2,1)S(1)}, f32[64,16,16,256]{3,0,2,1:T(8,128)}) fusion(f32[64]{0:T(128)S(1)} %copy-done.9, bf16[64,16,16,256]{3,2,1,0:T(8,128)(2,1)} %param.6, bf16[64,64]{1,0:T(8,128)(2,1)S(1)} %copy-done, f32[256,16,16,64,1]{0,3,4,2,1:T(8,128)} %fusion.27), kind=kOutput, calls=%fused_computation.30 | convolution fusion | flops 574357504 | bytes 42475776 | tf_op jit(solution)/shard_map/cyzx,co->oyzx/dot_general | solution.py:173
  367.0 38.8 %fusion.2 = bf16[64,16,16,256]{3,0,2,1:T(8,128)(2,1)S(1)} fusion(f32[64,16,16,256]{3,0,2,1:T(8,128)} %get-tuple-element.128, u16[64,16,256]{2,0,1:T(8,128)(2,1)S(1)} %get-tuple-element.127), kind=kLoop, calls=%fused_computation.4 | loop fusion | flops 285212672 | bytes 25690112 | tf_op jit(solution)/shard_map/convert_element_type | solution.py:177
  405.8 1.2 fusion.39
  407.1 2.2 collective-permute-start
  409.2 1.3 collective-permute-start.1
  410.6 1.9 collective-permute-done.1
  412.6 2.5 collective-permute-start.3
  415.1 1.3 collective-permute-start.2
  416.4 1.5 collective-permute-done.3
  417.9 4.7 collective-permute-done.2
  423.5 1.4 fusion.41
  424.9 1.0 fusion.44
  425.9 4.9 add_multiply_fusion
  430.8 1.3 negate_multiply_fusion.3
  432.1 1.1 negate_multiply_fusion.1
  433.3 2.8 slice_multiply_fusion.1
  436.1 1.0 add_add_fusion
  437.7 1.5 pad_add_fusion.1
  439.3 3.9 fusion.168
  443.2 0.8 fusion.175
  444.1 11.2 %convert_reduce_fusion = (f32[64]{0:T(128)S(1)}, bf16[64,16,16,256]{3,0,2,1:T(8,128)(2,1)S(1)}) fusion(f32[64,16,16,256]{3,0,2,1:T(8,128)S(1)} %bitcast.132, f32[16,16,256]{2,1,0:T(8,128)S(1)} %bitcast.135, f32[64]{0:T(128)S(1)} %get-tuple-element.125, f32[16,16,256]{2,1,0:T(8,128)S(1)} %bitcast.136, f32[64]{0:T(128)S(1)} %get-tuple-element.126, ...), kind=kLoop, calls=%fused_computation.15 | loop fusion | flops 71303104 | bytes 25953280 | tf_op jit(solution)/shard_map/reduce_sum | solution.py:217
  455.3 3.4 copy-done.3
  458.7 4.1 convert_bitcast_fusion
  462.8 6.3 copy.91
  469.1 7.2 reshape.339
  476.3 4.6 fusion.106
  480.9 4.7 fusion.111
  485.6 18.6 %slice_add_fusion.1 = (f32[32,16,32,64]{3,0,2,1:T(8,128)}, f32[32,16,32,64]{3,0,2,1:T(8,128)}) fusion(f32[32,16,32,128]{3,0,2,1:T(8,128)} %fusion.106, f32[32,16,32,128]{3,0,2,1:T(8,128)} %fusion.111), kind=kLoop, calls=%fused_computation.34 | loop fusion | flops 2097152 | bytes 25165824 | tf_op jit(solution)/shard_map/add | solution.py:44
  504.2 11.2 %pad_maximum_fusion.1 = f32[32,16,32,128]{3,0,2,1:T(8,128)} fusion(f32[32,16,32,64]{3,0,2,1:T(8,128)} %get-tuple-element.66, f32[32,16,32,64]{3,0,2,1:T(8,128)} %get-tuple-element.65), kind=kLoop, calls=%fused_computation.38 | loop fusion | flops 2097152 | bytes 16777216 | tf_op jit(solution)/shard_map/concatenate | solution.py:44
  515.4 11.5 %copy.67 = f32[32,16,32,128]{3,2,1,0:T(8,128)} copy(f32[32,16,32,128]{3,0,2,1:T(8,128)} %pad_maximum_fusion.1) | data formatting | bytes 16777216 | tf_op jit(solution)/shard_map/concatenate | solution.py:44
  527.0 108.1 %reduce-scatter.9.cloned.1.call-done = f32[2,16,32,128]{3,2,1,0:T(8,128)} async-done(((f32[32,16,32,128]{3,2,1,0:T(8,128)}), f32[2,16,32,128]{3,2,1,0:T(8,128)}) %reduce-scatter.9.cloned.1.call-update) | async-done | bytes 524304 | tf_op jit(solution)/shard_map/reduce_scatter | solution.py:90
  635.1 1.1 convert_element_type.176
  638.1 1.6 copy.70
  640.4 9.0 %convolution_bitcast_fusion.2 = f32[64,3]{0,1:T(4,128)S(1)} fusion(bf16[64,16,16,256]{3,0,2,1:T(8,128)(2,1)} %copy-done.2, f32[3,16,16,256]{3,0,2,1:T(4,128)S(1)} %get-tuple-element.35), kind=kOutput, calls=%fused_computation.91 | convolution fusion | flops 150994944 | bytes 9175808 | tf_op jit(solution)/shard_map/cyzx,byzx->cb/dot_general | solution.py:208
  649.4 15.3 %fusion.45 = f32[64,64]{0,1:T(8,128)S(1)} fusion(bf16[64,16,16,256]{3,0,2,1:T(8,128)(2,1)} %copy-done.3, bf16[64,16,16,256]{3,2,1,0:T(8,128)(2,1)} %param.6), kind=kOutput, calls=%fused_computation.90 | convolution fusion | flops 536870912 | bytes 16793600 | tf_op jit(solution)/shard_map/iyzx,oyzx->io/dot_general | solution.py:216
  664.8 66.2 %all-reduce.20 = (f32[]{:T(128)}, f32[64,64]{0,1:T(8,128)S(1)}, f32[64]{0:T(128)S(1)}, f32[64,3]{0,1:T(4,128)S(1)}, f32[3]{0:T(128)S(1)}) all-reduce(f32[]{:T(128)} %slice_reduce_fusion, f32[64,64]{0,1:T(8,128)S(1)} %fusion.45, f32[64]{0:T(128)S(1)} %get-tuple-element.36, ...), channel_id=1, replica_groups=mesh['gy'=16,'gz'=8] {'gy'}, use_global_device_ids=true, to_apply=%region_3.4 | all-reduce | flops 4356 | bytes 34848 | tf_op jit(solution)/shard_map/psum | solution.py:219
  731.0 36.1 %all-reduce.21 = (f32[]{:T(128)}, f32[64,64]{0,1:T(8,128)S(1)}, f32[64]{0:T(128)}, f32[64,3]{0,1:T(4,128)}, f32[3]{0:T(128)}) all-reduce(f32[]{:T(128)} %get-tuple-element.24, f32[64,64]{0,1:T(8,128)S(1)} %get-tuple-element.25, f32[64]{0:T(128)S(1)} %get-tuple-element.26, ...), channel_id=1, replica_groups=mesh['gy'=16,'gz'=8] {'gz'}, use_global_device_ids=true, to_apply=%region_4.5 | all-reduce | flops 4356 | bytes 34848 | tf_op jit(solution)/shard_map/psum | solution.py:218
  768.5 0.9 convert_convert_fusion
  769.4 8.5 %broadcast_multiply_fusion.1 = (f32[4,2,32,64,128]{4,3,2,1,0:T(8,128)}, f32[4,2,32,64,128]{4,3,2,1,0:T(8,128)}) fusion(f32[4,2,32,128]{3,2,1,0:T(8,128)S(1)} %convert_convert_fusion, f32[4,2,32,64]{3,2,1,0:T(8,128)S(1)} %copy-done.5, f32[4,2,32,64]{3,2,1,0:T(8,128)S(1)} %copy-done.6), kind=kLoop, calls=%fused_computation.56 | loop fusion | flops 4194304 | bytes 17039360 | tf_op jit(solution)/shard_map/abki,abko->abkio/dot_general | solution.py:142
  777.8 19.8 %slice_add_fusion = (f32[4,2,32,64,64]{4,3,2,1,0:T(8,128)}, f32[4,2,32,64,64]{4,3,2,1,0:T(8,128)}) fusion(f32[4,2,32,64,128]{4,3,2,1,0:T(8,128)} %get-tuple-element.119, f32[4,2,32,64,128]{4,3,2,1,0:T(8,128)} %get-tuple-element.118), kind=kLoop, calls=%fused_computation.32 | loop fusion | flops 2097152 | bytes 25165824 | tf_op jit(solution)/shard_map/add | solution.py:150
  797.7 12.1 %pad_maximum_fusion.2 = f32[4,2,32,64,128]{4,3,2,1,0:T(8,128)} fusion(f32[4,2,32,64,64]{4,3,2,1,0:T(8,128)} %get-tuple-element.64, f32[4,2,32,64,64]{4,3,2,1,0:T(8,128)} %get-tuple-element.63), kind=kLoop, calls=%fused_computation.39 | loop fusion | flops 2097152 | bytes 16777216 | tf_op jit(solution)/shard_map/concatenate | solution.py:148
  (77 shorter events, 10.5 us)
Async XLA Ops:
  7.2 340.5 %copy-start = (bf16[64,64]{1,0:T(8,128)(2,1)S(1)}, bf16[64,64]{1,0:T(8,128)(2,1)}, u32[]{:S(2)}) copy-start(bf16[64,64]{1,0:T(8,128)(2,1)} %param.8) | copy-start | bytes 24580
  7.2 183.6 %reduce-scatter.5.cloned.1.call-start = ((), (), s32[]{:S(2)}) async-start(), calls=%async_computation.4 | async-start | bytes 8912896 | tf_op jit(solution)/shard_map/reduce_scatter | solution.py:90
  85.8 148.4 %reduce-scatter.7.cloned.1.call-start = ((), (), s32[]{:S(2)}) async-start(), calls=%async_computation.5 | async-start | bytes 1179648 | tf_op jit(solution)/shard_map/reduce_scatter | solution.py:98
  195.3 133.3 %all-gather.2.cloned.1.call-start = ((), (), s32[]{:S(2)}) async-start(), calls=%async_computation.6 | async-start | bytes 4456448 | tf_op jit(solution)/shard_map/all_gather | solution.py:110
  274.4 360.8 %reduce-scatter.9.cloned.1.call-start = ((), (), s32[]{:S(2)}) async-start(), calls=%async_computation.7 | async-start | bytes 8912896 | tf_op jit(solution)/shard_map/reduce_scatter | solution.py:90
  328.6 4.9 copy-start.4
  339.5 8.1 copy-start.9
  367.0 38.8 %copy-start.7 = (bf16[64,3]{0,1:T(4,128)(2,1)S(1)}, bf16[64,3]{0,1:T(4,128)(2,1)}, u32[]{:S(2)}) copy-start(bf16[64,3]{0,1:T(4,128)(2,1)} %param.10) | copy-start | bytes 1156
  367.0 38.8 %copy-start.8 = (f32[3]{0:T(128)S(1)}, f32[3]{0:T(128)}, u32[]{:S(2)}) copy-start(f32[3]{0:T(128)} %param.11) | copy-start | bytes 40
  405.8 6.8 copy-start.2
  407.1 3.5 collective-permute-start
  409.2 3.2 collective-permute-start.1
  412.6 5.3 collective-permute-start.3
  415.1 7.5 collective-permute-start.2
  432.1 12.0 %slice-start = ((s8[16777216]{0:T(1024)(128)(4,1)}), s8[4194304]{0:T(1024)(128)(4,1)S(1)}, s32[]{:S(2)}) async-start(s8[16777216]{0:T(1024)(128)(4,1)} %bitcast.131), calls=%async_computation.9 | async-start | bytes 8388608
  433.3 10.8 %slice-start.1 = ((s8[16777216]{0:T(1024)(128)(4,1)}), s8[4194304]{0:T(1024)(128)(4,1)S(1)}, s32[]{:S(2)}) async-start(s8[16777216]{0:T(1024)(128)(4,1)} %bitcast.131), calls=%async_computation.10 | async-start | bytes 8388608
  437.7 6.4 slice-start.2
  439.3 4.8 slice-start.3
  455.3 3.4 copy-start.3
  527.0 241.5 %reduce-scatter.11.cloned.1.call-start = ((), (), s32[]{:S(2)}) async-start(), calls=%async_computation.8 | async-start | bytes 1179648 | tf_op jit(solution)/shard_map/reduce_scatter | solution.py:98
  649.4 120.0 %copy-start.5 = (f32[4,2,32,64]{3,2,1,0:T(8,128)S(1)}, f32[4,2,32,64]{3,2,1,0:T(8,128)}, u32[]{:S(2)}) copy-start(f32[4,2,32,64]{3,2,1,0:T(8,128)} %get-tuple-element.120) | copy-start | bytes 196612
  649.4 120.0 %copy-start.6 = (f32[4,2,32,64]{3,2,1,0:T(8,128)S(1)}, f32[4,2,32,64]{3,2,1,0:T(8,128)}, u32[]{:S(2)}) copy-start(f32[4,2,32,64]{3,2,1,0:T(8,128)} %get-tuple-element.121) | copy-start | bytes 196612
  797.7 12.1 %copy-start.1 = (bf16[64,64]{1,0:T(8,128)(2,1)S(1)}, bf16[64,64]{1,0:T(8,128)(2,1)}, u32[]{:S(2)}) copy-start(bf16[64,64]{1,0:T(8,128)(2,1)} %param.8) | copy-start | bytes 24580
Sparse Core Ops, SparseCore 0:
  85.9 104.8 reduce-scatter.4
  195.5 38.6 reduce-scatter.6
  274.5 54.0 all-gather.1
  527.1 107.9 reduce-scatter.8
  639.8 38.5 reduce-scatter.10
